TPU v7x, 32 devices: a whole 2x2x4 slice. The times are simulated.
32 devices in a mesh: dp: 16 (over z, y, core), fsdp: 2 (over x).
Axes of the slice: x: 2, y: 2, z: 4, core: 2. Of those that a mesh axis runs over, the one named last changes fastest.
Arguments:
- hidden_in: bfloat16 [4096, 1024], P(('dp', 'fsdp')), may hold values from -6 to 6
- doc_id: int32 [4096], P(('dp', 'fsdp')), may hold values from 0 to 128, as said below
- expert_ids: int32 [4096, 8], P(('dp', 'fsdp')), may hold values from 0 to 15, all different within a row
- out_grad: bfloat16 [4096, 1024], P(('dp', 'fsdp')), may hold values from -6 to 6
- attn_gain: bfloat16 [1024], P(('dp', 'fsdp')), may hold values from 0.5 to 1.5
- query_weight: bfloat16 [1024, 1024], P(('dp', 'fsdp')), may hold values from -0.1875 to 0.1875
- key_weight: bfloat16 [1024, 512], P(('dp', 'fsdp')), may hold values from -0.1875 to 0.1875
- value_weight: bfloat16 [1024, 512], P(('dp', 'fsdp')), may hold values from -0.1875 to 0.1875
- output_weight: bfloat16 [1024, 1024], P(('dp', 'fsdp')), may hold values from -0.75 to 0.75
- ffn_gain: bfloat16 [1024], P(('dp', 'fsdp')), may hold values from 0.5 to 1.5
- router_weight: bfloat16 [1024, 16], P(('dp', 'fsdp')), may hold values from -0.375 to 0.375
- expert_gate: bfloat16 [16, 1024, 512], P('dp', 'fsdp'), may hold values from -0.1875 to 0.1875
- expert_up: bfloat16 [16, 1024, 512], P('dp', 'fsdp'), may hold values from -0.1875 to 0.1875
- expert_down: bfloat16 [16, 512, 1024], P('dp', 'fsdp'), may hold values from -1 to 1
Outputs:
- layer_out: bfloat16 [4096, 1024], P(('dp', 'fsdp'))
- grad_in: bfloat16 [4096, 1024], P(('dp', 'fsdp'))
- grad_attn_gain: float32 [1024], P(('dp', 'fsdp'))
- grad_query: float32 [1024, 1024], P(('dp', 'fsdp'))
- grad_key: float32 [1024, 512], P(('dp', 'fsdp'))
- grad_value: float32 [1024, 512], P(('dp', 'fsdp'))
- grad_output: float32 [1024, 1024], P(('dp', 'fsdp'))
- grad_ffn_gain: float32 [1024], P(('dp', 'fsdp'))
- grad_router: float32 [1024, 16], P(('dp', 'fsdp'))
- grad_expert_gate: float32 [16, 1024, 512], P('dp', 'fsdp')
- grad_expert_up: float32 [16, 1024, 512], P('dp', 'fsdp')
- grad_expert_down: float32 [16, 512, 1024], P('dp', 'fsdp')
Inputs may be any that keep to these rules, and one draw needn't show every extreme that they name: Within each block of 128 rows doc_id starts at 0 and never falls; live rows come first and carry ids below 128; the rows after them carry 128 (padding). Every block has 64 or more live rows and some block has no padding. `expert_ids`: each row names 8 different experts.
All inputs are finite; a program needn't handle non-finite values.
Results may differ from a plain program's by a relative error of at most 0.015.
The roundings to bfloat16 on the way count: a program that leaves them out, or rounds other values in their place, can miss the bound.
Values may be sent and summed in bfloat16 or wider, within the bound.
A program may use at most 128 MiB of HBM per device.

v0:
```python
import jax
import jax.numpy as jnp
from jax import lax
from jax.sharding import PartitionSpec as P

HEADS = 16
KV_HEADS = 8
HEAD_DIM = 64
TOP = 8
CAP = 24
norm_eps = 1e-05


def positions_mask(doc_block):
    row_count = doc_block.shape[0]
    row_index = jnp.arange(row_count)
    same_doc = doc_block[:, None] == doc_block[None, :]
    earlier = row_index[None, :] < row_index[:, None]
    position = jnp.sum((same_doc & earlier).astype(jnp.float32), axis=1)
    allowed = same_doc & (row_index[None, :] <= row_index[:, None])
    live_rows = (doc_block < row_count).astype(jnp.float32)
    return (position, allowed, live_rows)


def rope_tables(position):
    half_dim = HEAD_DIM // 2
    freqs = jnp.exp(-jnp.log(10000.0) * (2.0 * jnp.arange(half_dim, dtype=jnp.float32) / HEAD_DIM))
    angle = position[:, None] * freqs[None, :]
    return (jnp.cos(angle), jnp.sin(angle))


def rotate(values, cosine, sinusoid):
    half_dim = values.shape[-1] // 2
    first_half, second_half = (values[..., :half_dim], values[..., half_dim:])
    return jnp.concatenate(
        [
            first_half * cosine - second_half * sinusoid,
            second_half * cosine + first_half * sinusoid,
        ],
        axis=-1,
    )


def unrotate(values, cosine, sinusoid):
    half_dim = values.shape[-1] // 2
    first_half, second_half = (values[..., :half_dim], values[..., half_dim:])
    return jnp.concatenate(
        [
            first_half * cosine + second_half * sinusoid,
            second_half * cosine - first_half * sinusoid,
        ],
        axis=-1,
    )


def norm_forward(values, gain):
    scale_row = lax.rsqrt(jnp.mean(values * values, axis=-1, keepdims=True) + norm_eps)
    normed = values * scale_row
    return (normed, scale_row, (normed * gain).astype(jnp.bfloat16))


def norm_backward(upstream, normed, scale_row, gain):
    scaled = upstream * gain
    inner = jnp.mean(scaled * normed, axis=-1, keepdims=True)
    return (scale_row * (scaled - normed * inner), jnp.sum(upstream * normed, axis=0))


def probabilities(query_b, key_b, allowed, log_total):
    scores = jnp.einsum(
        "ikgd,jkd->kgij", query_b, key_b, preferred_element_type=jnp.float32
    ) * HEAD_DIM ** (-0.5)
    raised = jnp.where(allowed[None, None], jnp.exp(scores), 0.0)
    if log_total is None:
        log_total = jnp.log(jnp.sum(raised, axis=-1, keepdims=True))
    return (jnp.where(allowed[None, None], jnp.exp(scores - log_total), 0.0), log_total)


def routing(expert_block, live_rows, logits):
    experts = logits.shape[1]
    row_count = expert_block.shape[0]
    chosen = jnp.sum(
        (expert_block[:, :, None] == jnp.arange(experts)[None, None, :]).astype(jnp.float32), axis=1
    )
    raised = jnp.where(chosen > 0, jnp.exp(logits), 0.0)
    gates = raised / jnp.sum(raised, axis=1, keepdims=True)
    member = chosen * live_rows[:, None]
    lower = (jnp.arange(row_count)[None, :] < jnp.arange(row_count)[:, None]).astype(jnp.float32)
    rank = jnp.dot(lower, member, precision=lax.Precision.HIGHEST)
    kept = member * (rank < CAP).astype(jnp.float32)
    slot_match = (rank.T[:, None, :] == jnp.arange(CAP, dtype=jnp.float32)[None, :, None]).astype(
        jnp.float32
    )
    dispatch = kept.T[:, None, :] * slot_match
    return (gates, dispatch, kept, rank)


def expert_forward(rows_in, w_gate, w_up, w_down):
    gate_pre = jnp.dot(rows_in, w_gate, preferred_element_type=jnp.float32)
    up_pre = jnp.dot(rows_in, w_up, preferred_element_type=jnp.float32)
    act_rows = (jax.nn.silu(gate_pre) * up_pre).astype(jnp.bfloat16)
    out_rows = jnp.dot(act_rows, w_down, preferred_element_type=jnp.float32).astype(jnp.bfloat16)
    return (gate_pre, up_pre, act_rows, out_rows)


def expert_backward(rows_in, gate_pre, up_pre, act_rows, grad_rows, w_gate, w_up, w_down):
    grad_act = jnp.dot(grad_rows, w_down.T, preferred_element_type=jnp.float32)
    sigmoid_gate = jax.nn.sigmoid(gate_pre)
    grad_up_pre = (grad_act * gate_pre * sigmoid_gate).astype(jnp.bfloat16)
    grad_gate_pre = (
        grad_act * up_pre * sigmoid_gate * (1.0 + gate_pre * (1.0 - sigmoid_gate))
    ).astype(jnp.bfloat16)
    grad_down_w = jnp.dot(act_rows.T, grad_rows, preferred_element_type=jnp.float32)
    grad_gate_w = jnp.dot(rows_in.T, grad_gate_pre, preferred_element_type=jnp.float32)
    grad_up_w = jnp.dot(rows_in.T, grad_up_pre, preferred_element_type=jnp.float32)
    grad_rows_in = jnp.dot(grad_gate_pre, w_gate.T, preferred_element_type=jnp.float32)
    grad_rows_in = (
        grad_rows_in + jnp.dot(grad_up_pre, w_up.T, preferred_element_type=jnp.float32)
    ).astype(jnp.bfloat16)
    return (grad_rows_in, grad_gate_w, grad_up_w, grad_down_w)


def shards(
    hidden_in,
    doc_id,
    expert_ids,
    out_grad,
    attn_gain,
    query_weight,
    key_weight,
    value_weight,
    output_weight,
    ffn_gain,
    router_weight,
    expert_gate,
    expert_up,
    expert_down,
):
    rows = hidden_in.shape[0]
    groups = HEADS // KV_HEADS
    scale = HEAD_DIM ** (-0.5)
    dense_full = (
        lax.all_gather(attn_gain, ("dp", "fsdp"), axis=0, tiled=True),
        lax.all_gather(query_weight, ("dp", "fsdp"), axis=0, tiled=True),
        lax.all_gather(key_weight, ("dp", "fsdp"), axis=0, tiled=True),
        lax.all_gather(value_weight, ("dp", "fsdp"), axis=0, tiled=True),
        lax.all_gather(output_weight, ("dp", "fsdp"), axis=0, tiled=True),
        lax.all_gather(ffn_gain, ("dp", "fsdp"), axis=0, tiled=True),
        lax.all_gather(router_weight, ("dp", "fsdp"), axis=0, tiled=True),
    )
    expert_full = (
        lax.all_gather(expert_gate, "fsdp", axis=1, tiled=True),
        lax.all_gather(expert_up, "fsdp", axis=1, tiled=True),
        lax.all_gather(expert_down, "fsdp", axis=1, tiled=True),
    )
    gain_one, w_query, w_key, w_value, w_output, gain_two, w_router = dense_full
    w_gate, w_up, w_down = (expert_full[0][0], expert_full[1][0], expert_full[2][0])
    position, allowed, live_rows = positions_mask(doc_id)
    cosine, sinusoid = rope_tables(position)
    cos_query, sin_query = (cosine[:, None, None, :], sinusoid[:, None, None, :])
    cos_key, sin_key = (cosine[:, None, :], sinusoid[:, None, :])
    resid_in = hidden_in.astype(jnp.float32)
    normed_one, scale_one, normed_in = norm_forward(resid_in, gain_one.astype(jnp.float32))
    query_raw = jnp.dot(normed_in, w_query, preferred_element_type=jnp.float32).reshape(
        rows, KV_HEADS, groups, HEAD_DIM
    )
    key_raw = jnp.dot(normed_in, w_key, preferred_element_type=jnp.float32).reshape(
        rows, KV_HEADS, HEAD_DIM
    )
    query_b = rotate(query_raw, cos_query, sin_query).astype(jnp.bfloat16)
    key_b = rotate(key_raw, cos_key, sin_key).astype(jnp.bfloat16)
    value_b = (
        jnp.dot(normed_in, w_value, preferred_element_type=jnp.float32)
        .reshape(rows, KV_HEADS, HEAD_DIM)
        .astype(jnp.bfloat16)
    )
    probs, log_total = probabilities(query_b, key_b, allowed, None)
    probs_b = probs.astype(jnp.bfloat16)
    mixed = jnp.einsum("kgij,jkd->ikgd", probs_b, value_b, preferred_element_type=jnp.float32)
    mixed_b = (
        (mixed * live_rows[:, None, None, None])
        .reshape(rows, HEADS * HEAD_DIM)
        .astype(jnp.bfloat16)
    )
    resid_mid = resid_in + jnp.dot(mixed_b, w_output, preferred_element_type=jnp.float32)
    normed_two, scale_two, routed_in = norm_forward(resid_mid, gain_two.astype(jnp.float32))
    logits = jnp.dot(routed_in, w_router, preferred_element_type=jnp.float32)
    gates, dispatch, kept, rank = routing(expert_ids, live_rows, logits)
    dispatch_b = dispatch.astype(jnp.bfloat16)
    send_rows = jnp.einsum(
        "ecr,rd->ecd", dispatch_b, routed_in, preferred_element_type=jnp.float32
    ).astype(jnp.bfloat16)
    recv_rows = lax.all_to_all(send_rows, "dp", split_axis=0, concat_axis=0, tiled=True)
    flat_in = recv_rows.reshape(-1, recv_rows.shape[2])
    gate_pre, up_pre, act_rows, out_rows = expert_forward(flat_in, w_gate, w_up, w_down)
    back_rows = lax.all_to_all(
        out_rows.reshape(recv_rows.shape), "dp", split_axis=0, concat_axis=0, tiled=True
    )
    experts = back_rows.shape[0]
    capacity = back_rows.shape[1]
    width = back_rows.shape[2]
    chosen_slot = (expert_ids[:, :, None] == jnp.arange(experts)[None, None, :]).astype(jnp.float32)
    gate_pick = jnp.sum(chosen_slot * (gates * kept)[:, None, :], axis=2)
    rank_pick = jnp.sum(chosen_slot * rank[:, None, :], axis=2)
    slot_index = expert_ids * capacity + jnp.minimum(rank_pick, capacity - 1.0).astype(jnp.int32)
    back_flat = back_rows.reshape(experts * capacity, width)
    picked_rows = jnp.take(back_flat, slot_index.reshape(-1), axis=0).reshape(rows, TOP, width)
    expert_sum = jnp.sum(gate_pick[:, :, None] * picked_rows.astype(jnp.float32), axis=1)
    layer_out = (resid_mid + expert_sum).astype(jnp.bfloat16)
    dense_full = (
        lax.all_gather(attn_gain, ("dp", "fsdp"), axis=0, tiled=True),
        lax.all_gather(query_weight, ("dp", "fsdp"), axis=0, tiled=True),
        lax.all_gather(key_weight, ("dp", "fsdp"), axis=0, tiled=True),
        lax.all_gather(value_weight, ("dp", "fsdp"), axis=0, tiled=True),
        lax.all_gather(output_weight, ("dp", "fsdp"), axis=0, tiled=True),
        lax.all_gather(ffn_gain, ("dp", "fsdp"), axis=0, tiled=True),
        lax.all_gather(router_weight, ("dp", "fsdp"), axis=0, tiled=True),
    )
    expert_full = (
        lax.all_gather(expert_gate, "fsdp", axis=1, tiled=True),
        lax.all_gather(expert_up, "fsdp", axis=1, tiled=True),
        lax.all_gather(expert_down, "fsdp", axis=1, tiled=True),
    )
    gain_one, w_query, w_key, w_value, w_output, gain_two, w_router = dense_full
    w_gate, w_up, w_down = (expert_full[0][0], expert_full[1][0], expert_full[2][0])
    grad_out = out_grad.astype(jnp.float32)
    slot_gate = jnp.sum(dispatch * gates.T[:, None, :], axis=2)
    pulled_grad = jnp.einsum(
        "ecr,rd->ecd", dispatch_b, out_grad, preferred_element_type=jnp.float32
    )
    grad_send = (slot_gate[:, :, None] * pulled_grad).astype(jnp.bfloat16)
    slot_dot = jnp.sum(back_rows.astype(jnp.float32) * pulled_grad, axis=2)
    grad_gates = jnp.sum(dispatch * slot_dot[:, :, None], axis=1).T
    grad_logits = gates * (grad_gates - jnp.sum(gates * grad_gates, axis=1, keepdims=True))
    grad_logits_b = grad_logits.astype(jnp.bfloat16)
    grad_recv = lax.all_to_all(grad_send, "dp", split_axis=0, concat_axis=0, tiled=True)
    grad_rows_in, grad_gate_w, grad_up_w, grad_down_w = expert_backward(
        flat_in, gate_pre, up_pre, act_rows, grad_recv.reshape(flat_in.shape), w_gate, w_up, w_down
    )
    grad_back = lax.all_to_all(
        grad_rows_in.reshape(recv_rows.shape), "dp", split_axis=0, concat_axis=0, tiled=True
    )
    grad_routed = jnp.einsum(
        "ecr,ecd->rd", dispatch_b, grad_back, preferred_element_type=jnp.float32
    )
    grad_routed = grad_routed + jnp.dot(
        grad_logits_b, w_router.T, preferred_element_type=jnp.float32
    )
    grad_w_router = jnp.dot(routed_in.T, grad_logits_b, preferred_element_type=jnp.float32)
    grad_norm_two, grad_gain_two = norm_backward(
        grad_routed, normed_two, scale_two, gain_two.astype(jnp.float32)
    )
    grad_mid = grad_out + grad_norm_two
    grad_mid_b = grad_mid.astype(jnp.bfloat16)
    grad_w_output = jnp.dot(mixed_b.T, grad_mid_b, preferred_element_type=jnp.float32)
    grad_mixed = jnp.dot(grad_mid_b, w_output.T, preferred_element_type=jnp.float32).reshape(
        rows, KV_HEADS, groups, HEAD_DIM
    )
    grad_mixed = (grad_mixed * live_rows[:, None, None, None]).astype(jnp.bfloat16)
    probs_again, unused_total = probabilities(query_b, key_b, allowed, log_total)
    grad_probs = jnp.einsum(
        "ikgd,jkd->kgij", grad_mixed, value_b, preferred_element_type=jnp.float32
    )
    delta = jnp.sum(probs_again * grad_probs, axis=-1, keepdims=True)
    grad_scores = (probs_again * (grad_probs - delta) * scale).astype(jnp.bfloat16)
    grad_query_raw = jnp.einsum(
        "kgij,jkd->ikgd", grad_scores, key_b, preferred_element_type=jnp.float32
    )
    grad_key_raw = jnp.einsum(
        "kgij,ikgd->jkd", grad_scores, query_b, preferred_element_type=jnp.float32
    )
    grad_value_raw = jnp.einsum(
        "kgij,ikgd->jkd",
        probs_again.astype(jnp.bfloat16),
        grad_mixed,
        preferred_element_type=jnp.float32,
    )
    grad_query_b = (
        unrotate(grad_query_raw, cos_query, sin_query)
        .reshape(rows, HEADS * HEAD_DIM)
        .astype(jnp.bfloat16)
    )
    grad_key_b = (
        unrotate(grad_key_raw, cos_key, sin_key)
        .reshape(rows, KV_HEADS * HEAD_DIM)
        .astype(jnp.bfloat16)
    )
    grad_value_b = grad_value_raw.reshape(rows, KV_HEADS * HEAD_DIM).astype(jnp.bfloat16)
    grad_w_query = jnp.dot(normed_in.T, grad_query_b, preferred_element_type=jnp.float32)
    grad_w_key = jnp.dot(normed_in.T, grad_key_b, preferred_element_type=jnp.float32)
    grad_w_value = jnp.dot(normed_in.T, grad_value_b, preferred_element_type=jnp.float32)
    grad_normed = jnp.dot(grad_query_b, w_query.T, preferred_element_type=jnp.float32)
    grad_normed = grad_normed + jnp.dot(grad_key_b, w_key.T, preferred_element_type=jnp.float32)
    grad_normed = grad_normed + jnp.dot(grad_value_b, w_value.T, preferred_element_type=jnp.float32)
    grad_norm_one, grad_gain_one = norm_backward(
        grad_normed, normed_one, scale_one, gain_one.astype(jnp.float32)
    )
    grad_input = (grad_mid + grad_norm_one).astype(jnp.bfloat16)
    dense_grads = (
        lax.psum_scatter(grad_gain_one, ("dp", "fsdp"), scatter_dimension=0, tiled=True),
        lax.psum_scatter(grad_w_query, ("dp", "fsdp"), scatter_dimension=0, tiled=True),
        lax.psum_scatter(grad_w_key, ("dp", "fsdp"), scatter_dimension=0, tiled=True),
        lax.psum_scatter(grad_w_value, ("dp", "fsdp"), scatter_dimension=0, tiled=True),
        lax.psum_scatter(grad_w_output, ("dp", "fsdp"), scatter_dimension=0, tiled=True),
        lax.psum_scatter(grad_gain_two, ("dp", "fsdp"), scatter_dimension=0, tiled=True),
        lax.psum_scatter(grad_w_router, ("dp", "fsdp"), scatter_dimension=0, tiled=True),
    )
    expert_grads = (
        lax.psum_scatter(
            grad_gate_w[None].astype(jnp.bfloat16), "fsdp", scatter_dimension=1, tiled=True
        ).astype(jnp.float32),
        lax.psum_scatter(
            grad_up_w[None].astype(jnp.bfloat16), "fsdp", scatter_dimension=1, tiled=True
        ).astype(jnp.float32),
        lax.psum_scatter(
            grad_down_w[None].astype(jnp.bfloat16), "fsdp", scatter_dimension=1, tiled=True
        ).astype(jnp.float32),
    )
    return (
        layer_out,
        grad_input,
        dense_grads[0],
        dense_grads[1],
        dense_grads[2],
        dense_grads[3],
        dense_grads[4],
        dense_grads[5],
        dense_grads[6],
        expert_grads[0],
        expert_grads[1],
        expert_grads[2],
    )


def solution(mesh):
    in_specs = (
        P(("dp", "fsdp"), None),
        P(("dp", "fsdp")),
        P(("dp", "fsdp"), None),
        P(("dp", "fsdp"), None),
        P(("dp", "fsdp")),
        P(("dp", "fsdp"), None),
        P(("dp", "fsdp"), None),
        P(("dp", "fsdp"), None),
        P(("dp", "fsdp"), None),
        P(("dp", "fsdp")),
        P(("dp", "fsdp"), None),
        P("dp", "fsdp", None),
        P("dp", "fsdp", None),
        P("dp", "fsdp", None),
    )
    out_specs = (
        P(("dp", "fsdp"), None),
        P(("dp", "fsdp"), None),
        P(("dp", "fsdp")),
        P(("dp", "fsdp"), None),
        P(("dp", "fsdp"), None),
        P(("dp", "fsdp"), None),
        P(("dp", "fsdp"), None),
        P(("dp", "fsdp")),
        P(("dp", "fsdp"), None),
        P("dp", "fsdp", None),
        P("dp", "fsdp", None),
        P("dp", "fsdp", None),
    )
    return jax.shard_map(shards, mesh=mesh, in_specs=in_specs, out_specs=out_specs, check_vma=False)
```

profile of v0, /device:TPU:0, one launch (start us, length us, event | category | flops | bytes accessed | tf_op | source)
XLA Modules:
  0.0 1174.7 jit_solution(4902561280423588323)
XLA Ops:
  11.8 0.8 convert_reduce_fusion.1
  12.7 0.8 compare_and_fusion.1
  13.5 0.8 dynamic-update-slice
  14.4 0.8 dynamic-update-slice.1
  15.2 41.9 %all-reduce.5 = (bf16[1024]{0:T(1024)(128)(2,1)S(1)}, bf16[1024]{0:T(1024)(128)(2,1)S(1)}) all-reduce(bf16[1024]{0:T(1024)(128)(2,1)S(1)} %dynamic-update-slice, bf16[1024]{0:T(1024)(128)(2,1)S(1)} %dynamic-update-slice.1), channel_id=1, replica_groups=mesh['dp'=16,'fsdp'=2] {'dp','fsdp'}, use_global_device_ids=true, to_apply=%add | all-reduce | flops 2048 | bytes 8192
  57.1 1.1 fusion.44
  59.3 8.2 all-gather.9.cloned.1.call-done
  67.5 1.7 convolution_convert_fusion.5
  69.3 54.0 %all-gather.11.cloned.1.call-done = bf16[1024,512]{1,0:T(8,128)(2,1)} async-done(((bf16[32,512]{1,0:T(8,128)(2,1)}), bf16[1024,512]{1,0:T(8,128)(2,1)}) %all-gather.11.cloned.1.call-update) | async-done | bytes 1048592 | tf_op jit(solution)/shard_map/all_gather | solution.py:144
  123.2 1.8 fusion.99
  125.1 56.5 %all-gather.13.cloned.1.call-done = bf16[1024,1024]{1,0:T(8,128)(2,1)} async-done(((bf16[32,1024]{1,0:T(8,128)(2,1)}), bf16[1024,1024]{1,0:T(8,128)(2,1)}) %all-gather.13.cloned.1.call-update) | async-done | bytes 2097168 | tf_op jit(solution)/shard_map/all_gather | solution.py:143
  181.6 2.6 fusion.97
  185.5 54.2 %all-gather.15.cloned.1.call-done = bf16[1024,1024]{1,0:T(8,128)(2,1)} async-done(((bf16[32,1024]{1,0:T(8,128)(2,1)}), bf16[1024,1024]{1,0:T(8,128)(2,1)}) %all-gather.15.cloned.1.call-update) | async-done | bytes 2097168 | tf_op jit(solution)/shard_map/all_gather | solution.py:146
  239.7 2.1 multiply_reduce_fusion.5
  242.8 1.2 convolution_convert_fusion.4
  244.0 4.5 all-to-all-start
  249.2 12.0 %all-gather.17.cloned.1.call-done = bf16[1,1024,512]{2,1,0:T(8,128)(2,1)} async-done(((bf16[1,512,512]{2,1,0:T(8,128)(2,1)}), bf16[1,1024,512]{2,1,0:T(8,128)(2,1)}) %all-gather.17.cloned.1.call-update) | async-done | bytes 1048592 | tf_op jit(solution)/shard_map/all_gather | solution.py:151
  261.2 5.9 all-to-all-done
  267.1 1.8 fusion.25
  268.9 15.0 %all-gather.19.cloned.1.call-done = bf16[1,1024,512]{2,1,0:T(8,128)(2,1)} async-done(((bf16[1,512,512]{2,1,0:T(8,128)(2,1)}), bf16[1,1024,512]{2,1,0:T(8,128)(2,1)}) %all-gather.19.cloned.1.call-update) | async-done | bytes 1048592 | tf_op jit(solution)/shard_map/all_gather | solution.py:152
  284.0 2.7 multiply_convert_fusion.3
  286.6 20.2 %all-gather.21.cloned.1.call-done = bf16[1,512,1024]{2,1,0:T(8,128)(2,1)} async-done(((bf16[1,256,1024]{2,1,0:T(8,128)(2,1)}), bf16[1,512,1024]{2,1,0:T(8,128)(2,1)}) %all-gather.21.cloned.1.call-update) | async-done | bytes 1048592 | tf_op jit(solution)/shard_map/all_gather | solution.py:153
  306.8 2.8 convolution_convert_fusion.3
  309.6 5.6 all-to-all-start.1
  315.2 76.2 %all-gather = bf16[32,32,16]{1,2,0:T(8,128)(2,1)S(1)} all-gather(bf16[1,32,16]{1,2,0:T(8,128)(2,1)S(1)} %bitcast.165), channel_id=1, replica_groups=mesh['dp'=16,'fsdp'=2] {'dp','fsdp'}, dimensions={0}, use_global_device_ids=true | all-gather | bytes 33792 | tf_op jit(solution)/shard_map/all_gather | solution.py:148
  392.5 1.1 multiply_convert_fusion
  393.6 3.6 all-to-all-start.2
  397.9 1.1 fusion.104
  399.0 16.8 %all-to-all-done.2 = bf16[16,24,1024]{2,1,0:T(8,128)(2,1)S(1)} async-done(((bf16[16,24,1024]{2,1,0:T(8,128)(2,1)}), bf16[16,24,1024]{2,1,0:T(8,128)(2,1)S(1)}, u32[]{:S(2)}, u32[]{:S(2)}) %all-to-all-start.2) | async-done | bytes 786464 | tf_op jit(solution)/shard_map/all_to_all | solution.py:235
  415.8 2.8 multiply_convert_fusion.1
  419.4 1.7 fusion.2
  421.2 1.7 fusion.3
  423.0 1.7 fusion.23
  424.7 1.5 add_convert_fusion
  426.2 5.7 all-to-all-start.3
  432.0 1.3 fusion.11
  433.9 4.1 gather_fusion
  438.0 2.3 multiply_reduce_fusion
  440.3 1.7 fusion.4
  442.1 8.6 all-to-all-done.3
  450.7 1.5 convolution_bitcast_fusion.2
  452.2 0.9 multiply_reduce_fusion.3
  453.1 0.9 multiply_add_fusion
  455.4 2.1 convolution_bitcast_fusion.4
  457.6 1.9 fusion.93
  459.6 2.1 fusion.15
  461.6 1.9 fusion.91
  463.6 2.1 convolution_bitcast_fusion.1
  465.8 2.8 fusion.95
  468.7 0.9 copy-done.17
  469.6 2.7 fusion.56
  472.3 65.3 %reduce-scatter.25.cloned.1.call-done = f32[32,16]{1,0:T(8,128)} async-done(((f32[1024,16]{1,0:T(8,128)}), f32[32,16]{1,0:T(8,128)}) %reduce-scatter.25.cloned.1.call-update) | async-done | bytes 2064
  537.6 1.4 copy.93
  539.0 0.8 fusion.103
  541.4 38.1 %all-reduce.4 = (f32[1024]{0:T(1024)S(1)}, f32[1024]{0:T(1024)S(1)}) all-reduce(f32[1024]{0:T(1024)S(1)} %get-tuple-element.14, f32[1024]{0:T(1024)S(1)} %copy-done.49), channel_id=2, replica_groups=mesh['dp'=16,'fsdp'=2] {'dp','fsdp'}, use_global_device_ids=true, to_apply=%region_17.18.clone | all-reduce | flops 2048 | bytes 16384
  580.6 0.9 fusion.42
  581.6 2.1 convert_element_type.188
  583.7 2.1 convert_element_type.191
  585.9 17.1 %reduce-scatter.23.cloned.1.call-done = bf16[1,256,1024]{2,1,0:T(8,128)(2,1)} async-done(((bf16[1,512,1024]{2,1,0:T(8,128)(2,1)}), bf16[1,256,1024]{2,1,0:T(8,128)(2,1)}) %reduce-scatter.23.cloned.1.call-update) | async-done | bytes 524304 | tf_op jit(solution)/shard_map/reduce_scatter | solution.py:314
  602.9 2.1 convert_element_type.194
  605.0 139.8 %reduce-scatter.13.cloned.1.call-done = f32[32,512]{1,0:T(8,128)} async-done(((f32[1024,512]{1,0:T(8,128)}), f32[32,512]{1,0:T(8,128)}) %reduce-scatter.13.cloned.1.call-update) | async-done | bytes 65552 | tf_op jit(solution)/shard_map/reduce_scatter | solution.py:301
  744.9 137.4 %reduce-scatter.15.cloned.1.call-done = f32[32,512]{1,0:T(8,128)} async-done(((f32[1024,512]{1,0:T(8,128)}), f32[32,512]{1,0:T(8,128)}) %reduce-scatter.15.cloned.1.call-update) | async-done | bytes 65552 | tf_op jit(solution)/shard_map/reduce_scatter | solution.py:302
  882.3 142.9 %reduce-scatter.11.cloned.1.call-done = f32[32,1024]{1,0:T(8,128)} async-done(((f32[1024,1024]{1,0:T(8,128)}), f32[32,1024]{1,0:T(8,128)}) %reduce-scatter.11.cloned.1.call-update) | async-done | bytes 131088 | tf_op jit(solution)/shard_map/reduce_scatter | solution.py:300
  1025.2 143.0 %reduce-scatter.17.cloned.1.call-done = f32[32,1024]{1,0:T(8,128)} async-done(((f32[1024,1024]{1,0:T(8,128)}), f32[32,1024]{1,0:T(8,128)}) %reduce-scatter.17.cloned.1.call-update) | async-done | bytes 131088 | tf_op jit(solution)/shard_map/reduce_scatter | solution.py:303
  (191 shorter events, 16.1 us)
Async XLA Ops:
  7.2 116.1 %copy-start = (bf16[128,1024]{1,0:T(8,128)(2,1)S(1)}, bf16[128,1024]{1,0:T(8,128)(2,1)}, u32[]{:S(2)}) copy-start(bf16[128,1024]{1,0:T(8,128)(2,1)} %param.14) | copy-start | bytes 786436
  7.2 60.3 %all-gather.9.cloned.1.call-start = ((), (), s32[]{:S(2)}) async-start(), calls=%async_computation.12 | async-start | bytes 1081344 | tf_op jit(solution)/shard_map/all_gather | solution.py:145
  7.9 115.3 %all-gather.11.cloned.1.call-start = ((), (), s32[]{:S(2)}) async-start(), calls=%async_computation.13 | async-start | bytes 1081344 | tf_op jit(solution)/shard_map/all_gather | solution.py:144
  8.7 172.9 %all-gather.13.cloned.1.call-start = ((), (), s32[]{:S(2)}) async-start(), calls=%async_computation.14 | async-start | bytes 2162688 | tf_op jit(solution)/shard_map/all_gather | solution.py:143
  9.4 230.3 %all-gather.15.cloned.1.call-start = ((), (), s32[]{:S(2)}) async-start(), calls=%async_computation.15 | async-start | bytes 2162688 | tf_op jit(solution)/shard_map/all_gather | solution.py:146
  10.0 251.3 %all-gather.17.cloned.1.call-start = ((), (), s32[]{:S(2)}) async-start(), calls=%async_computation.16 | async-start | bytes 1572864 | tf_op jit(solution)/shard_map/all_gather | solution.py:151
  10.6 273.4 %all-gather.19.cloned.1.call-start = ((), (), s32[]{:S(2)}) async-start(), calls=%async_computation.17 | async-start | bytes 1572864 | tf_op jit(solution)/shard_map/all_gather | solution.py:152
  11.8 385.4 %copy-start.55 = (f32[128]{0:T(128)}, f32[128]{0:T(128)S(1)}, u32[]{:S(2)}) copy-start(f32[128]{0:T(128)S(1)} %compare_convert_fusion) | copy-start | bytes 1540
  13.5 171.5 %copy-start.50 = (pred[128,128]{0,1:T(8,128)(4,1)}, pred[128,128]{0,1:T(8,128)(4,1)S(1)}, u32[]{:S(2)}) copy-start(pred[128,128]{0,1:T(8,128)(4,1)S(1)} %compare_and_fusion.1) | copy-start | bytes 49156
  57.1 127.1 %copy-start.29 = (f32[1024]{0:T(1024)}, f32[1024]{0:T(1024)S(1)}, u32[]{:S(2)}) copy-start(f32[1024]{0:T(1024)S(1)} %convert_element_type.150) | copy-start | bytes 12292
  58.2 126.0 %copy-start.47 = (f32[128]{0:T(128)}, f32[128]{0:T(128)S(1)}, u32[]{:S(2)}) copy-start(f32[128]{0:T(128)S(1)} %add_rsqrt_fusion.1) | copy-start | bytes 1540
  58.2 183.6 %copy-start.41 = (f32[1024]{0:T(1024)}, f32[1024]{0:T(1024)S(1)}, u32[]{:S(2)}) copy-start(f32[1024]{0:T(1024)S(1)} %convert_element_type.161) | copy-start | bytes 12292
  59.1 125.1 %copy-start.25 = (f32[128,32]{0,1:T(8,128)}, f32[128,32]{0,1:T(8,128)S(1)}, u32[]{:S(2)}) copy-start(f32[128,32]{0,1:T(8,128)S(1)} %get-tuple-element.41) | copy-start | bytes 49156
  59.2 333.1 %copy-start.39 = (f32[16,128]{1,0:T(8,128)}, f32[16,128]{1,0:T(8,128)S(1)}, u32[]{:S(2)}) copy-start(f32[16,128]{1,0:T(8,128)S(1)} %get-tuple-element.42) | copy-start | bytes 24580
  59.2 338.0 %copy-start.33 = (f32[128,16]{0,1:T(8,128)}, f32[128,16]{0,1:T(8,128)S(1)}, u32[]{:S(2)}) copy-start(f32[128,16]{0,1:T(8,128)S(1)} %get-tuple-element.43) | copy-start | bytes 24580
  69.3 115.7 %copy-start.19 = (bf16[128,512]{0,1:T(8,128)(2,1)}, bf16[128,512]{0,1:T(8,128)(2,1)S(1)}, u32[]{:S(2)}) copy-start(bf16[128,512]{0,1:T(8,128)(2,1)S(1)} %copy.69) | copy-start | bytes 393220
  125.1 59.5 %copy-start.35 = (bf16[128,8,32]{0,2,1:T(8,128)(2,1)}, bf16[128,8,32]{0,2,1:T(8,128)(2,1)S(1)}, u32[]{:S(2)}) copy-start(bf16[128,8,32]{0,2,1:T(8,128)(2,1)S(1)} %get-tuple-element.36) | copy-start | bytes 196612
  125.1 59.5 %copy-start.37 = (bf16[128,8,32]{0,2,1:T(8,128)(2,1)}, bf16[128,8,32]{0,2,1:T(8,128)(2,1)S(1)}, u32[]{:S(2)}) copy-start(bf16[128,8,32]{0,2,1:T(8,128)(2,1)S(1)} %get-tuple-element.37) | copy-start | bytes 196612
  185.0 56.9 %copy-start.13 = (f32[8,2,128,128]{2,3,1,0:T(8,128)}, f32[8,2,128,128]{2,3,1,0:T(8,128)S(1)}, u32[]{:S(2)}) copy-start(f32[8,2,128,128]{2,3,1,0:T(8,128)S(1)} %fusion.12) | copy-start | bytes 3145732
  185.5 58.5 %copy-start.16 = (bf16[8,64,2,128]{3,1,2,0:T(8,128)(2,1)}, bf16[8,64,2,128]{3,1,2,0:T(8,128)(2,1)S(1)}, u32[]{:S(2)}) copy-start(bf16[8,64,2,128]{3,1,2,0:T(8,128)(2,1)S(1)} %fusion.14) | copy-start | bytes 786436
  241.9 2.1 copy-start.52
  244.0 23.2 %all-to-all-start = ((bf16[16,24,1024]{2,1,0:T(8,128)(2,1)}), bf16[16,24,1024]{2,1,0:T(8,128)(2,1)S(1)}, u32[]{:S(2)}, u32[]{:S(2)}) async-start(bf16[16,24,1024]{2,1,0:T(8,128)(2,1)} %convolution_convert_fusion.4), calls=%async_computation | async-start | bytes 1572864 | tf_op jit(solution)/shard_map/all_to_all | solution.py:192
  248.5 58.3 %all-gather.21.cloned.1.call-start = ((), (), s32[]{:S(2)}) async-start(), calls=%async_computation.18 | async-start | bytes 1572864 | tf_op jit(solution)/shard_map/all_gather | solution.py:153
  268.9 17.7 %copy-start.18 = (f32[384,512]{1,0:T(8,128)}, f32[384,512]{1,0:T(8,128)S(1)}, u32[]{:S(2)}) copy-start(f32[384,512]{1,0:T(8,128)S(1)} %fusion.25) | copy-start | bytes 2359300
  286.6 28.6 %copy-start.27 = (bf16[384,512]{1,0:T(8,128)(2,1)}, bf16[384,512]{1,0:T(8,128)(2,1)S(1)}, u32[]{:S(2)}) copy-start(bf16[384,512]{1,0:T(8,128)(2,1)S(1)} %get-tuple-element.46) | copy-start | bytes 1179652
  286.6 28.6 %copy-start.54 = (bf16[32,16]{0,1:T(8,128)(2,1)S(1)}, bf16[32,16]{0,1:T(8,128)(2,1)}, u32[]{:S(2)}) copy-start(bf16[32,16]{0,1:T(8,128)(2,1)} %param.24) | copy-start | bytes 3076
  306.8 85.0 %copy-start.12 = (bf16[128,1024]{1,0:T(8,128)(2,1)S(1)}, bf16[128,1024]{1,0:T(8,128)(2,1)}, u32[]{:S(2)}) copy-start(bf16[128,1024]{1,0:T(8,128)(2,1)} %param.17) | copy-start | bytes 786436
  309.6 82.3 %all-to-all-start.1 = ((bf16[16,24,1024]{2,1,0:T(8,128)(2,1)}), bf16[16,24,1024]{2,1,0:T(8,128)(2,1)S(1)}, u32[]{:S(2)}, u32[]{:S(2)}) async-start(bf16[16,24,1024]{2,1,0:T(8,128)(2,1)} %bitcast.18), calls=%async_computation.1 | async-start | bytes 1572864 | tf_op jit(solution)/shard_map/all_to_all | solution.py:195
  391.6 2.0 copy-start.31
  393.6 22.3 %all-to-all-start.2 = ((bf16[16,24,1024]{2,1,0:T(8,128)(2,1)}), bf16[16,24,1024]{2,1,0:T(8,128)(2,1)S(1)}, u32[]{:S(2)}, u32[]{:S(2)}) async-start(bf16[16,24,1024]{2,1,0:T(8,128)(2,1)} %multiply_convert_fusion), calls=%async_computation.2 | async-start | bytes 1572864 | tf_op jit(solution)/shard_map/all_to_all | solution.py:235
  397.2 140.4 %reduce-scatter.25.cloned.1.call-start = ((), (), s32[]{:S(2)}) async-start(), calls=%async_computation.26 | async-start | bytes 540672
  397.9 17.9 %copy-start.43 = (bf16[128,16]{0,1:T(8,128)(2,1)}, bf16[128,16]{0,1:T(8,128)(2,1)S(1)}, u32[]{:S(2)}) copy-start(bf16[128,16]{0,1:T(8,128)(2,1)S(1)} %get-tuple-element.38) | copy-start | bytes 12292
  399.0 182.6 %reduce-scatter.19.cloned.1.call-start = ((), (), s32[]{:S(2)}) async-start(), calls=%async_computation.23 | async-start | bytes 1572864 | tf_op jit(solution)/shard_map/reduce_scatter | solution.py:308
  415.8 2.8 copy-start.8
  421.1 1.8 copy-start.5
  421.2 162.6 %reduce-scatter.21.cloned.1.call-start = ((), (), s32[]{:S(2)}) async-start(), calls=%async_computation.24 | async-start | bytes 1572864 | tf_op jit(solution)/shard_map/reduce_scatter | solution.py:311
  424.7 7.4 copy-start.14
  424.7 7.4 copy-start.51
  426.2 7.1 copy-start.34
  426.2 7.1 copy-start.45
  426.2 7.1 copy-start.46
  426.2 24.5 %all-to-all-start.3 = ((bf16[16,24,1024]{2,1,0:T(8,128)(2,1)}), bf16[16,24,1024]{2,1,0:T(8,128)(2,1)}, u32[]{:S(2)}, u32[]{:S(2)}) async-start(bf16[16,24,1024]{2,1,0:T(8,128)(2,1)} %bitcast.25), calls=%async_computation.3 | async-start | bytes 1572864 | tf_op jit(solution)/shard_map/all_to_all | solution.py:239
  432.0 170.9 %reduce-scatter.23.cloned.1.call-start = ((), (), s32[]{:S(2)}) async-start(), calls=%async_computation.25 | async-start | bytes 1572864 | tf_op jit(solution)/shard_map/reduce_scatter | solution.py:314
  437.9 2.3 copy-start.9
  437.9 2.3 copy-start.28
  440.3 10.4 copy-start.40
  440.3 11.9 %copy-start.4 = (f32[128,1024]{1,0:T(8,128)S(1)}, f32[128,1024]{1,0:T(8,128)}, u32[]{:S(2)}) copy-start(f32[128,1024]{1,0:T(8,128)} %copy-done.3) | copy-start | bytes 1572868
  440.3 11.9 %copy-start.32 = (bf16[1024,16]{0,1:T(8,128)(2,1)S(1)}, bf16[1024,16]{0,1:T(8,128)(2,1)}, u32[]{:S(2)}) copy-start(bf16[1024,16]{0,1:T(8,128)(2,1)} %copy-done.31) | copy-start | bytes 98308
  440.3 11.9 %copy-start.42 = (f32[1024]{0:T(1024)S(1)}, f32[1024]{0:T(1024)}, u32[]{:S(2)}) copy-start(f32[1024]{0:T(1024)} %copy-done.41) | copy-start | bytes 12292
  440.3 11.9 %copy-start.44 = (bf16[128,16]{0,1:T(8,128)(2,1)S(1)}, bf16[128,16]{0,1:T(8,128)(2,1)}, u32[]{:S(2)}) copy-start(bf16[128,16]{0,1:T(8,128)(2,1)} %copy-done.43) | copy-start | bytes 12292
  440.3 11.9 %copy-start.53 = (f32[128]{0:T(128)S(1)}, f32[128]{0:T(128)}, u32[]{:S(2)}) copy-start(f32[128]{0:T(128)} %copy-done.52) | copy-start | bytes 1540
  442.0 11.1 copy-start.10
  442.1 302.8 %reduce-scatter.13.cloned.1.call-start = ((), (), s32[]{:S(2)}) async-start(), calls=%async_computation.20 | async-start | bytes 2162688 | tf_op jit(solution)/shard_map/reduce_scatter | solution.py:301
  452.2 1.9 copy-start.2
  454.8 2.7 copy-start.26
  454.8 2.7 copy-start.30
  454.8 2.7 copy-start.48
  459.5 422.8 %reduce-scatter.15.cloned.1.call-start = ((), (), s32[]{:S(2)}) async-start(), calls=%async_computation.21 | async-start | bytes 2162688 | tf_op jit(solution)/shard_map/reduce_scatter | solution.py:302
  461.6 1.9 copy-start.36
  461.6 1.9 copy-start.38
  463.5 561.6 %reduce-scatter.11.cloned.1.call-start = ((), (), s32[]{:S(2)}) async-start(), calls=%async_computation.19 | async-start | bytes 4325376 | tf_op jit(solution)/shard_map/reduce_scatter | solution.py:300
  468.6 699.5 %reduce-scatter.17.cloned.1.call-start = ((), (), s32[]{:S(2)}) async-start(), calls=%async_computation.22 | async-start | bytes 4325376 | tf_op jit(solution)/shard_map/reduce_scatter | solution.py:303
  472.3 66.7 %copy-start.1 = (bf16[1024,1024]{1,0:T(8,128)(2,1)S(1)}, bf16[1024,1024]{1,0:T(8,128)(2,1)}, u32[]{:S(2)}) copy-start(bf16[1024,1024]{1,0:T(8,128)(2,1)} %all-gather.13.cloned.1.call-done) | copy-start | bytes 6291460
  539.0 1.7 copy-start.6
  (12 other events, 12.2 us)
Sparse Core Ops, SparseCore 0:
  10.9 56.5 all-gather.8
  70.4 52.8 all-gather.10
  126.2 55.3 all-gather.12
  184.4 55.1 all-gather.14
  241.1 20.1 all-gather.16
  262.6 21.2 all-gather.18
  285.5 21.2 all-gather.20
  400.3 137.3 reduce-scatter.24
  540.4 17.0 reduce-scatter.18
  559.6 20.5 reduce-scatter.20
  582.4 20.4 reduce-scatter.22
  605.6 139.2 reduce-scatter.12
  747.7 134.5 reduce-scatter.14
  885.0 140.1 reduce-scatter.10
  1027.9 140.2 reduce-scatter.16
where the time goes:
time: 1180 us; the launch traced here: 1170 us
  waiting for transfers between devices  901 us (76%)
  blocking collectives  156 us (13%)
  matrix products  51.4 us (4%)
  starting transfers between devices  20 us (2%)
  other arithmetic  18.5 us (2%)
  between operations  14.8 us (1%)
  local copies, waits for them, and re-layouts  12.5 us (1%)
    reduce_scatter x1, waiting for transfers between devices, shards(): lax.psum_scatter(grad_w_output, ('dp', 'fsdp'), scatter_dimension=0, tile...  143 us
    reduce_scatter x1, waiting for transfers between devices, shards(): lax.psum_scatter(grad_w_query, ('dp', 'fsdp'), scatter_dimension=0, tiled...  143 us
    reduce_scatter x1, waiting for transfers between devices, shards(): lax.psum_scatter(grad_w_key, ('dp', 'fsdp'), scatter_dimension=0, tiled=T...  140 us
    reduce_scatter x1, waiting for transfers between devices, shards(): lax.psum_scatter(grad_w_value, ('dp', 'fsdp'), scatter_dimension=0, tiled...  137 us
    unnamed x2, blocking collectives  80 us
    all_gather x1, blocking collectives, shards(): lax.all_gather(router_weight, ('dp', 'fsdp'), axis=0, tiled=True)  76.2 us
    unnamed x16, waiting for transfers between devices  69.8 us
    all_gather x1, waiting for transfers between devices, shards(): lax.all_gather(query_weight, ('dp', 'fsdp'), axis=0, tiled=True)  56.5 us
  transfers between devices with their start and end apart: 19, of which 16 were waited for; matrix products, arithmetic and copies ran while one was open for 6% of the time, Pallas kernels for 0%

commit v1 on v0

--- a/solution.py
+++ b/solution.py
@@ -9,6 +9,28 @@
 TOP = 8
 CAP = 24
 norm_eps = 1e-05
+
+
+def laid_out(tiles, dim):
+    shape = list(tiles.shape[1:])
+    shape[dim] *= tiles.shape[0]
+    return jnp.moveaxis(tiles, 0, dim).reshape(shape)
+
+
+def grow_blocks(value, axis):
+    peers = lax.axis_size(axis)
+    parts = value[None]
+    for level in range(peers.bit_length() - 1):
+        bit = 1 << level
+        received = lax.ppermute(parts, axis, [(i, i ^ bit) for i in range(peers)])
+        both = jnp.stack([parts, received])
+        upper = lax.axis_index(axis) >> level & 1
+        parts = jnp.where(upper == 0, both, both[::-1]).reshape(-1, *value.shape)
+    return parts
+
+
+def doubled_up(array, axis, dim):
+    return laid_out(grow_blocks(array, axis), dim)
 
 
 def positions_mask(doc_block):
@@ -145,7 +167,7 @@
         lax.all_gather(value_weight, ("dp", "fsdp"), axis=0, tiled=True),
         lax.all_gather(output_weight, ("dp", "fsdp"), axis=0, tiled=True),
         lax.all_gather(ffn_gain, ("dp", "fsdp"), axis=0, tiled=True),
-        lax.all_gather(router_weight, ("dp", "fsdp"), axis=0, tiled=True),
+        doubled_up(router_weight, ("dp", "fsdp"), 0),
     )
     expert_full = (
         lax.all_gather(expert_gate, "fsdp", axis=1, tiled=True),

time: 1180 us -> 1120 us (0.949)
  waiting for transfers between devices: 901 us -> 842 us
    unnamed x16, waiting for transfers between devices: 69.8 us -> 3.83 us
    ppermute x0 -> x5, waiting for transfers between devices: none -> 21.3 us  [grow_blocks(): received = lax.ppermute(parts, axis, [(i, i ^ bit) for i in range(peers)])]
  transfers between devices with their start and end apart: 19 -> 24, of which waited for: 16 -> 19; matrix products, arithmetic and copies ran while one was open for 6% -> 7% of each run, Pallas kernels for 0% -> 0%
where the time goes in v1:
time: 1120 us
  waiting for transfers between devices  842 us (75%)
  blocking collectives  151 us (13%)
  matrix products  52.1 us (5%)
  starting transfers between devices  28.1 us (3%)
  other arithmetic  18.6 us (2%)
  between operations  15 us (1%)
  local copies, waits for them, and re-layouts  14.6 us (1%)
    reduce_scatter x1, waiting for transfers between devices, shards(): lax.psum_scatter(grad_w_output, ('dp', 'fsdp'), scatter_dimension=0, tile...  143 us
    reduce_scatter x1, waiting for transfers between devices, shards(): lax.psum_scatter(grad_w_query, ('dp', 'fsdp'), scatter_dimension=0, tiled...  142 us
    reduce_scatter x1, waiting for transfers between devices, shards(): lax.psum_scatter(grad_w_key, ('dp', 'fsdp'), scatter_dimension=0, tiled=T...  140 us
    reduce_scatter x1, waiting for transfers between devices, shards(): lax.psum_scatter(grad_w_value, ('dp', 'fsdp'), scatter_dimension=0, tiled...  138 us
    unnamed x2, blocking collectives  82.5 us
    all_gather x1, blocking collectives, shards(): lax.all_gather(router_weight, ('dp', 'fsdp'), axis=0, tiled=True)  68.5 us
    all_gather x1, waiting for transfers between devices, shards(): lax.all_gather(query_weight, ('dp', 'fsdp'), axis=0, tiled=True)  56.5 us
    all_gather x1, waiting for transfers between devices, shards(): lax.all_gather(output_weight, ('dp', 'fsdp'), axis=0, tiled=True)  54.4 us
  transfers between devices with their start and end apart: 24, of which 19 were waited for; matrix products, arithmetic and copies ran while one was open for 7% of the time, Pallas kernels for 0%

profile of v1, /device:TPU:0, one launch (start us, length us, event | category | flops | bytes accessed | tf_op | source)
XLA Modules:
  0.0 1121.9 jit_solution(7467553408258319338)
XLA Ops:
  15.2 41.9 %all-reduce.5 = (bf16[1024]{0:T(1024)(128)(2,1)S(1)}, bf16[1024]{0:T(1024)(128)(2,1)S(1)}) all-reduce(bf16[1024]{0:T(1024)(128)(2,1)S(1)} %dynamic-update-slice, bf16[1024]{0:T(1024)(128)(2,1)S(1)} %dynamic-update-slice.1), channel_id=1, replica_groups=mesh['dp'=16,'fsdp'=2] {'dp','fsdp'}, use_global_device_ids=true, to_apply=%add | all-reduce | flops 2048 | bytes 8192
  57.1 1.1 fusion.44
  59.3 8.2 all-gather.9.cloned.1.call-done
  67.5 1.7 convolution_convert_fusion.5
  69.3 54.0 %all-gather.11.cloned.1.call-done = bf16[1024,512]{1,0:T(8,128)(2,1)} async-done(((bf16[32,512]{1,0:T(8,128)(2,1)}), bf16[1024,512]{1,0:T(8,128)(2,1)}) %all-gather.11.cloned.1.call-update) | async-done | bytes 1048592 | tf_op jit(solution)/shard_map/all_gather | solution.py:166
  123.2 1.8 fusion.103
  125.2 56.5 %all-gather.13.cloned.1.call-done = bf16[1024,1024]{1,0:T(8,128)(2,1)} async-done(((bf16[32,1024]{1,0:T(8,128)(2,1)}), bf16[1024,1024]{1,0:T(8,128)(2,1)}) %all-gather.13.cloned.1.call-update) | async-done | bytes 2097168 | tf_op jit(solution)/shard_map/all_gather | solution.py:165
  181.6 2.6 fusion.101
  185.2 54.4 %all-gather.15.cloned.1.call-done = bf16[1024,1024]{1,0:T(8,128)(2,1)} async-done(((bf16[32,1024]{1,0:T(8,128)(2,1)}), bf16[1024,1024]{1,0:T(8,128)(2,1)}) %all-gather.15.cloned.1.call-update) | async-done | bytes 2097168 | tf_op jit(solution)/shard_map/all_gather | solution.py:168
  239.7 2.1 multiply_reduce_fusion.5
  242.8 1.2 convolution_convert_fusion.4
  244.0 4.5 all-to-all-start
  249.3 3.2 collective-permute-done
  252.6 1.1 collective-permute-done.1
  253.7 2.0 collective-permute-start.2
  255.7 5.6 all-gather.17.cloned.1.call-done
  261.3 5.8 all-to-all-done
  267.2 1.8 fusion.25
  269.0 15.1 %all-gather.19.cloned.1.call-done = bf16[1,1024,512]{2,1,0:T(8,128)(2,1)} async-done(((bf16[1,512,512]{2,1,0:T(8,128)(2,1)}), bf16[1,1024,512]{2,1,0:T(8,128)(2,1)}) %all-gather.19.cloned.1.call-update) | async-done | bytes 1048592 | tf_op jit(solution)/shard_map/all_gather | solution.py:174
  284.0 2.7 multiply_convert_fusion.3
  286.7 20.2 %all-gather.21.cloned.1.call-done = bf16[1,512,1024]{2,1,0:T(8,128)(2,1)} async-done(((bf16[1,256,1024]{2,1,0:T(8,128)(2,1)}), bf16[1,512,1024]{2,1,0:T(8,128)(2,1)}) %all-gather.21.cloned.1.call-update) | async-done | bytes 1048592 | tf_op jit(solution)/shard_map/all_gather | solution.py:175
  306.9 2.7 convolution_convert_fusion.3
  309.6 5.8 all-to-all-start.1
  315.4 2.0 collective-permute-start.3
  317.4 12.4 %collective-permute-done.3 = bf16[8,32,16]{1,0,2:T(8,128)(2,1)S(1)} collective-permute-done((bf16[8,32,16]{1,0,2:T(8,128)(2,1)S(1)}, bf16[8,32,16]{1,0,2:T(8,128)(2,1)S(1)}, u32[]{:S(2)}, u32[]{:S(2)}) %collective-permute-start.3) | collective-permute-done | bytes 8224 | tf_op jit(solution)/shard_map/ppermute | solution.py:25
  329.8 4.6 collective-permute-start.4
  334.4 4.6 collective-permute-done.4
  340.2 1.0 multiply_convert_fusion
  341.2 3.6 all-to-all-start.2
  345.5 1.1 fusion.108
  346.7 16.8 %all-to-all-done.2 = bf16[16,24,1024]{2,1,0:T(8,128)(2,1)S(1)} async-done(((bf16[16,24,1024]{2,1,0:T(8,128)(2,1)}), bf16[16,24,1024]{2,1,0:T(8,128)(2,1)S(1)}, u32[]{:S(2)}, u32[]{:S(2)}) %all-to-all-start.2) | async-done | bytes 786464 | tf_op jit(solution)/shard_map/all_to_all | solution.py:257
  363.5 2.8 multiply_convert_fusion.1
  367.0 1.7 fusion.2
  368.8 68.5 %all-gather = bf16[32,32,16]{1,2,0:T(8,128)(2,1)S(1)} all-gather(bf16[1,32,16]{1,2,0:T(8,128)(2,1)} %bitcast.192), channel_id=1, replica_groups=mesh['dp'=16,'fsdp'=2] {'dp','fsdp'}, dimensions={0}, use_global_device_ids=true | all-gather | bytes 33792 | tf_op jit(solution)/shard_map/all_gather | solution.py:238
  438.0 1.7 reshape.319
  439.7 1.7 fusion.3
  441.5 1.7 fusion.23
  443.2 1.5 add_convert_fusion
  444.8 4.4 all-to-all-start.3
  449.3 1.3 fusion.11
  451.1 4.1 gather_fusion
  455.2 2.3 multiply_reduce_fusion
  457.5 1.7 fusion.4
  459.3 8.6 all-to-all-done.3
  467.9 1.5 convolution_bitcast_fusion.2
  469.8 0.9 multiply_add_fusion
  472.2 2.1 convolution_bitcast_fusion.4
  474.4 1.9 fusion.97
  476.4 2.1 fusion.15
  478.5 1.8 fusion.95
  480.5 2.1 convolution_bitcast_fusion.1
  482.7 2.8 fusion.99
  486.4 2.7 fusion.56
  489.2 1.5 copy.99
  491.7 1.8 convolution_add_fusion.1
  494.1 40.6 %all-reduce.4 = (f32[1024]{0:T(1024)S(1)}, f32[1024]{0:T(1024)S(1)}) all-reduce(f32[1024]{0:T(1024)S(1)} %get-tuple-element.14, f32[1024]{0:T(1024)S(1)} %get-tuple-element.12), channel_id=2, replica_groups=mesh['dp'=16,'fsdp'=2] {'dp','fsdp'}, use_global_device_ids=true, to_apply=%region_17.18.clone | all-reduce | flops 2048 | bytes 16384
  536.8 2.1 convert_element_type.188
  538.9 2.1 convert_element_type.191
  541.1 8.7 reduce-scatter.23.cloned.1.call-done
  549.8 2.1 convert_element_type.194
  551.9 139.9 %reduce-scatter.13.cloned.1.call-done = f32[32,512]{1,0:T(8,128)} async-done(((f32[1024,512]{1,0:T(8,128)}), f32[32,512]{1,0:T(8,128)}) %reduce-scatter.13.cloned.1.call-update) | async-done | bytes 65552 | tf_op jit(solution)/shard_map/reduce_scatter | solution.py:323
  691.8 137.9 %reduce-scatter.15.cloned.1.call-done = f32[32,512]{1,0:T(8,128)} async-done(((f32[1024,512]{1,0:T(8,128)}), f32[32,512]{1,0:T(8,128)}) %reduce-scatter.15.cloned.1.call-update) | async-done | bytes 65552 | tf_op jit(solution)/shard_map/reduce_scatter | solution.py:324
  829.7 142.4 %reduce-scatter.11.cloned.1.call-done = f32[32,1024]{1,0:T(8,128)} async-done(((f32[1024,1024]{1,0:T(8,128)}), f32[32,1024]{1,0:T(8,128)}) %reduce-scatter.11.cloned.1.call-update) | async-done | bytes 131088 | tf_op jit(solution)/shard_map/reduce_scatter | solution.py:322
  972.1 143.3 %reduce-scatter.17.cloned.1.call-done = f32[32,1024]{1,0:T(8,128)} async-done(((f32[1024,1024]{1,0:T(8,128)}), f32[32,1024]{1,0:T(8,128)}) %reduce-scatter.17.cloned.1.call-update) | async-done | bytes 131088 | tf_op jit(solution)/shard_map/reduce_scatter | solution.py:325
  (212 shorter events, 22.5 us)
Async XLA Ops:
  7.2 116.1 %copy-start = (bf16[128,1024]{1,0:T(8,128)(2,1)S(1)}, bf16[128,1024]{1,0:T(8,128)(2,1)}, u32[]{:S(2)}) copy-start(bf16[128,1024]{1,0:T(8,128)(2,1)} %param.14) | copy-start | bytes 786436
  7.2 60.3 %all-gather.9.cloned.1.call-start = ((), (), s32[]{:S(2)}) async-start(), calls=%async_computation.12 | async-start | bytes 1081344 | tf_op jit(solution)/shard_map/all_gather | solution.py:167
  7.9 115.3 %all-gather.11.cloned.1.call-start = ((), (), s32[]{:S(2)}) async-start(), calls=%async_computation.13 | async-start | bytes 1081344 | tf_op jit(solution)/shard_map/all_gather | solution.py:166
  8.7 172.9 %all-gather.13.cloned.1.call-start = ((), (), s32[]{:S(2)}) async-start(), calls=%async_computation.14 | async-start | bytes 2162688 | tf_op jit(solution)/shard_map/all_gather | solution.py:165
  9.4 230.3 %all-gather.15.cloned.1.call-start = ((), (), s32[]{:S(2)}) async-start(), calls=%async_computation.15 | async-start | bytes 2162688 | tf_op jit(solution)/shard_map/all_gather | solution.py:168
  10.0 251.3 %all-gather.17.cloned.1.call-start = ((), (), s32[]{:S(2)}) async-start(), calls=%async_computation.16 | async-start | bytes 1572864 | tf_op jit(solution)/shard_map/all_gather | solution.py:173
  10.6 273.5 %all-gather.19.cloned.1.call-start = ((), (), s32[]{:S(2)}) async-start(), calls=%async_computation.17 | async-start | bytes 1572864 | tf_op jit(solution)/shard_map/all_gather | solution.py:174
  11.8 333.1 %copy-start.54 = (f32[128]{0:T(128)}, f32[128]{0:T(128)S(1)}, u32[]{:S(2)}) copy-start(f32[128]{0:T(128)S(1)} %compare_convert_fusion) | copy-start | bytes 1540
  13.5 171.2 %copy-start.49 = (pred[128,128]{0,1:T(8,128)(4,1)}, pred[128,128]{0,1:T(8,128)(4,1)S(1)}, u32[]{:S(2)}) copy-start(pred[128,128]{0,1:T(8,128)(4,1)S(1)} %compare_and_fusion.1) | copy-start | bytes 49156
  57.1 127.1 %copy-start.30 = (f32[1024]{0:T(1024)}, f32[1024]{0:T(1024)S(1)}, u32[]{:S(2)}) copy-start(f32[1024]{0:T(1024)S(1)} %convert_element_type.150) | copy-start | bytes 12292
  58.2 126.0 %copy-start.47 = (f32[128]{0:T(128)}, f32[128]{0:T(128)S(1)}, u32[]{:S(2)}) copy-start(f32[128]{0:T(128)S(1)} %add_rsqrt_fusion.1) | copy-start | bytes 1540
  58.2 183.7 %copy-start.41 = (f32[1024]{0:T(1024)}, f32[1024]{0:T(1024)S(1)}, u32[]{:S(2)}) copy-start(f32[1024]{0:T(1024)S(1)} %convert_element_type.161) | copy-start | bytes 12292
  59.1 125.1 %copy-start.26 = (f32[128,32]{0,1:T(8,128)}, f32[128,32]{0,1:T(8,128)S(1)}, u32[]{:S(2)}) copy-start(f32[128,32]{0,1:T(8,128)S(1)} %get-tuple-element.45) | copy-start | bytes 49156
  59.2 280.7 %copy-start.39 = (f32[16,128]{1,0:T(8,128)}, f32[16,128]{1,0:T(8,128)S(1)}, u32[]{:S(2)}) copy-start(f32[16,128]{1,0:T(8,128)S(1)} %get-tuple-element.46) | copy-start | bytes 24580
  59.2 285.7 %copy-start.32 = (f32[128,16]{0,1:T(8,128)}, f32[128,16]{0,1:T(8,128)S(1)}, u32[]{:S(2)}) copy-start(f32[128,16]{0,1:T(8,128)S(1)} %get-tuple-element.47) | copy-start | bytes 24580
  69.3 115.4 %copy-start.20 = (bf16[128,512]{0,1:T(8,128)(2,1)}, bf16[128,512]{0,1:T(8,128)(2,1)S(1)}, u32[]{:S(2)}) copy-start(bf16[128,512]{0,1:T(8,128)(2,1)S(1)} %copy.73) | copy-start | bytes 393220
  125.1 59.5 %copy-start.34 = (bf16[128,8,32]{0,2,1:T(8,128)(2,1)}, bf16[128,8,32]{0,2,1:T(8,128)(2,1)S(1)}, u32[]{:S(2)}) copy-start(bf16[128,8,32]{0,2,1:T(8,128)(2,1)S(1)} %get-tuple-element.36) | copy-start | bytes 196612
  125.1 59.5 %copy-start.36 = (bf16[128,8,32]{0,2,1:T(8,128)(2,1)}, bf16[128,8,32]{0,2,1:T(8,128)(2,1)S(1)}, u32[]{:S(2)}) copy-start(bf16[128,8,32]{0,2,1:T(8,128)(2,1)S(1)} %get-tuple-element.37) | copy-start | bytes 196612
  184.3 57.5 %copy-start.22 = (bf16[128,8,2,32]{0,3,2,1:T(8,128)(2,1)}, bf16[128,8,2,32]{0,3,2,1:T(8,128)(2,1)S(1)}, u32[]{:S(2)}) copy-start(bf16[128,8,2,32]{0,3,2,1:T(8,128)(2,1)S(1)} %get-tuple-element.30) | copy-start | bytes 393220
  184.3 57.5 %copy-start.24 = (bf16[128,8,2,32]{0,3,2,1:T(8,128)(2,1)}, bf16[128,8,2,32]{0,3,2,1:T(8,128)(2,1)S(1)}, u32[]{:S(2)}) copy-start(bf16[128,8,2,32]{0,3,2,1:T(8,128)(2,1)S(1)} %get-tuple-element.31) | copy-start | bytes 393220
  184.7 57.2 %copy-start.14 = (f32[8,2,128,128]{2,3,1,0:T(8,128)}, f32[8,2,128,128]{2,3,1,0:T(8,128)S(1)}, u32[]{:S(2)}) copy-start(f32[8,2,128,128]{2,3,1,0:T(8,128)S(1)} %fusion.12) | copy-start | bytes 3145732
  185.2 58.8 %copy-start.17 = (bf16[8,64,2,128]{3,1,2,0:T(8,128)(2,1)}, bf16[8,64,2,128]{3,1,2,0:T(8,128)(2,1)S(1)}, u32[]{:S(2)}) copy-start(bf16[8,64,2,128]{3,1,2,0:T(8,128)(2,1)S(1)} %fusion.14) | copy-start | bytes 786436
  241.9 6.7 copy-start.51
  241.9 10.5 copy-start.52
  244.0 23.1 %all-to-all-start = ((bf16[16,24,1024]{2,1,0:T(8,128)(2,1)}), bf16[16,24,1024]{2,1,0:T(8,128)(2,1)S(1)}, u32[]{:S(2)}, u32[]{:S(2)}) async-start(bf16[16,24,1024]{2,1,0:T(8,128)(2,1)} %convolution_convert_fusion.4), calls=%async_computation | async-start | bytes 1572864 | tf_op jit(solution)/shard_map/all_to_all | solution.py:214
  248.5 58.4 %all-gather.21.cloned.1.call-start = ((), (), s32[]{:S(2)}) async-start(), calls=%async_computation.18 | async-start | bytes 1572864 | tf_op jit(solution)/shard_map/all_gather | solution.py:175
  248.6 3.9 collective-permute-start
  252.5 1.2 collective-permute-start.1
  253.7 61.6 %collective-permute-start.2 = (bf16[4,32,16]{1,2,0:T(8,128)(2,1)S(1)}, bf16[4,32,16]{1,2,0:T(8,128)(2,1)S(1)}, u32[]{:S(2)}, u32[]{:S(2)}) collective-permute-start(bf16[4,32,16]{1,2,0:T(8,128)(2,1)S(1)} %bitcast.188), channel_id=1, source_target_pairs={{0,4},{1,5},{2,6},{3,7},{4,0},{5,1},{6,2},{7,3},{8,12},{9,13},{10,... | collective-permute-start | bytes 12296 | tf_op jit(solution)/shard_map/ppermute | solution.py:25
  269.0 17.8 %copy-start.19 = (f32[384,512]{1,0:T(8,128)}, f32[384,512]{1,0:T(8,128)S(1)}, u32[]{:S(2)}) copy-start(f32[384,512]{1,0:T(8,128)S(1)} %fusion.25) | copy-start | bytes 2359300
  286.7 43.1 %copy-start.28 = (bf16[384,512]{1,0:T(8,128)(2,1)}, bf16[384,512]{1,0:T(8,128)(2,1)S(1)}, u32[]{:S(2)}) copy-start(bf16[384,512]{1,0:T(8,128)(2,1)S(1)} %get-tuple-element.50) | copy-start | bytes 1179652
  309.6 29.9 %copy-start.13 = (bf16[128,1024]{1,0:T(8,128)(2,1)S(1)}, bf16[128,1024]{1,0:T(8,128)(2,1)}, u32[]{:S(2)}) copy-start(bf16[128,1024]{1,0:T(8,128)(2,1)} %param.17) | copy-start | bytes 786436
  309.6 29.9 %all-to-all-start.1 = ((bf16[16,24,1024]{2,1,0:T(8,128)(2,1)}), bf16[16,24,1024]{2,1,0:T(8,128)(2,1)S(1)}, u32[]{:S(2)}, u32[]{:S(2)}) async-start(bf16[16,24,1024]{2,1,0:T(8,128)(2,1)} %bitcast.32), calls=%async_computation.1 | async-start | bytes 1572864 | tf_op jit(solution)/shard_map/all_to_all | solution.py:217
  315.4 14.4 %collective-permute-start.3 = (bf16[8,32,16]{1,0,2:T(8,128)(2,1)S(1)}, bf16[8,32,16]{1,0,2:T(8,128)(2,1)S(1)}, u32[]{:S(2)}, u32[]{:S(2)}) collective-permute-start(bf16[8,32,16]{1,0,2:T(8,128)(2,1)S(1)} %copy.77), channel_id=1, source_target_pairs={{0,8},{1,9},{2,10},{3,11},{4,12},{5,13},{6,14},{7,15},{8,0},{9,1},... | collective-permute-start | bytes 24584 | tf_op jit(solution)/shard_map/ppermute | solution.py:25
  329.8 9.2 collective-permute-start.4
  341.2 22.3 %all-to-all-start.2 = ((bf16[16,24,1024]{2,1,0:T(8,128)(2,1)}), bf16[16,24,1024]{2,1,0:T(8,128)(2,1)S(1)}, u32[]{:S(2)}, u32[]{:S(2)}) async-start(bf16[16,24,1024]{2,1,0:T(8,128)(2,1)} %multiply_convert_fusion), calls=%async_computation.2 | async-start | bytes 1572864 | tf_op jit(solution)/shard_map/all_to_all | solution.py:257
  344.8 144.4 %reduce-scatter.25.cloned.1.call-start = ((), (), s32[]{:S(2)}) async-start(), calls=%async_computation.26 | async-start | bytes 540672
  345.5 17.9 %copy-start.43 = (bf16[128,16]{0,1:T(8,128)(2,1)}, bf16[128,16]{0,1:T(8,128)(2,1)S(1)}, u32[]{:S(2)}) copy-start(bf16[128,16]{0,1:T(8,128)(2,1)S(1)} %get-tuple-element.40) | copy-start | bytes 12292
  346.6 190.2 %reduce-scatter.19.cloned.1.call-start = ((), (), s32[]{:S(2)}) async-start(), calls=%async_computation.23 | async-start | bytes 1572864 | tf_op jit(solution)/shard_map/reduce_scatter | solution.py:330
  363.5 2.8 copy-start.9
  368.8 72.7 %copy-start.7 = (bf16[1,1024,512]{2,1,0:T(8,128)(2,1)S(1)}, bf16[1,1024,512]{2,1,0:T(8,128)(2,1)}, u32[]{:S(2)}) copy-start(bf16[1,1024,512]{2,1,0:T(8,128)(2,1)} %all-gather.17.cloned.1.call-done) | copy-start | bytes 3145732
  368.8 170.2 %reduce-scatter.21.cloned.1.call-start = ((), (), s32[]{:S(2)}) async-start(), calls=%async_computation.24 | async-start | bytes 1572864 | tf_op jit(solution)/shard_map/reduce_scatter | solution.py:333
  443.2 6.0 copy-start.15
  443.2 6.0 copy-start.50
  444.8 5.8 copy-start.33
  444.8 5.8 copy-start.45
  444.8 5.8 copy-start.46
  444.8 23.1 %all-to-all-start.3 = ((bf16[16,24,1024]{2,1,0:T(8,128)(2,1)}), bf16[16,24,1024]{2,1,0:T(8,128)(2,1)}, u32[]{:S(2)}, u32[]{:S(2)}) async-start(bf16[16,24,1024]{2,1,0:T(8,128)(2,1)} %bitcast.39), calls=%async_computation.3 | async-start | bytes 1572864 | tf_op jit(solution)/shard_map/all_to_all | solution.py:261
  449.2 100.6 %reduce-scatter.23.cloned.1.call-start = ((), (), s32[]{:S(2)}) async-start(), calls=%async_computation.25 | async-start | bytes 1572864 | tf_op jit(solution)/shard_map/reduce_scatter | solution.py:336
  457.5 10.4 copy-start.40
  457.5 11.9 %copy-start.4 = (f32[128,1024]{1,0:T(8,128)S(1)}, f32[128,1024]{1,0:T(8,128)}, u32[]{:S(2)}) copy-start(f32[128,1024]{1,0:T(8,128)} %copy-done.3) | copy-start | bytes 1572868
  457.5 11.9 %copy-start.38 = (bf16[1024,16]{0,1:T(8,128)(2,1)S(1)}, bf16[1024,16]{0,1:T(8,128)(2,1)}, u32[]{:S(2)}) copy-start(bf16[1024,16]{0,1:T(8,128)(2,1)} %reshape.319) | copy-start | bytes 98308
  457.5 11.9 %copy-start.42 = (f32[1024]{0:T(1024)S(1)}, f32[1024]{0:T(1024)}, u32[]{:S(2)}) copy-start(f32[1024]{0:T(1024)} %copy-done.41) | copy-start | bytes 12292
  457.5 11.9 %copy-start.44 = (bf16[128,16]{0,1:T(8,128)(2,1)S(1)}, bf16[128,16]{0,1:T(8,128)(2,1)}, u32[]{:S(2)}) copy-start(bf16[128,16]{0,1:T(8,128)(2,1)} %copy-done.43) | copy-start | bytes 12292
  457.5 11.9 %copy-start.53 = (f32[128]{0:T(128)S(1)}, f32[128]{0:T(128)}, u32[]{:S(2)}) copy-start(f32[128]{0:T(128)} %copy-done.52) | copy-start | bytes 1540
  459.3 10.6 copy-start.11
  459.3 232.5 %reduce-scatter.13.cloned.1.call-start = ((), (), s32[]{:S(2)}) async-start(), calls=%async_computation.20 | async-start | bytes 2162688 | tf_op jit(solution)/shard_map/reduce_scatter | solution.py:323
  470.8 14.8 %copy-start.5 = (f32[128,1024]{1,0:T(8,128)}, f32[128,1024]{1,0:T(8,128)S(1)}, u32[]{:S(2)}) copy-start(f32[128,1024]{1,0:T(8,128)S(1)} %get-tuple-element.32) | copy-start | bytes 1572868
  471.8 2.6 copy-start.31
  471.8 2.6 copy-start.48
  476.4 353.3 %reduce-scatter.15.cloned.1.call-start = ((), (), s32[]{:S(2)}) async-start(), calls=%async_computation.21 | async-start | bytes 2162688 | tf_op jit(solution)/shard_map/reduce_scatter | solution.py:324
  480.4 491.7 %reduce-scatter.11.cloned.1.call-start = ((), (), s32[]{:S(2)}) async-start(), calls=%async_computation.19 | async-start | bytes 4325376 | tf_op jit(solution)/shard_map/reduce_scatter | solution.py:322
  485.5 629.9 %reduce-scatter.17.cloned.1.call-start = ((), (), s32[]{:S(2)}) async-start(), calls=%async_computation.22 | async-start | bytes 4325376 | tf_op jit(solution)/shard_map/reduce_scatter | solution.py:325
  491.7 44.2 %copy-start.6 = (f32[128,1024]{1,0:T(8,128)S(1)}, f32[128,1024]{1,0:T(8,128)}, u32[]{:S(2)}) copy-start(f32[128,1024]{1,0:T(8,128)} %copy-done.5) | copy-start | bytes 1572868
  (16 other events, 25.6 us)
Sparse Core Ops, SparseCore 0:
  10.9 56.5 all-gather.8
  70.4 52.8 all-gather.10
  126.2 55.3 all-gather.12
  184.4 55.1 all-gather.14
  241.1 20.2 all-gather.16
  262.7 21.2 all-gather.18
  285.6 21.2 all-gather.20
  347.9 136.7 reduce-scatter.24
  487.5 16.7 reduce-scatter.18
  506.4 20.6 reduce-scatter.20
  529.4 20.3 reduce-scatter.22
  552.5 139.2 reduce-scatter.12
  694.6 134.9 reduce-scatter.14
  832.4 139.6 reduce-scatter.10
  974.8 140.5 reduce-scatter.16
